TPU v7x, 128 devices: a whole 4x4x4 slice. The times are simulated.
128 devices in a mesh: side: 2 (over core), grp: 8 (over x_hi, y), tp: 8 (over x_lo, z).
Axes of the slice: x: 4 (x_hi: 2, x_lo: 2; x = x_hi * 2 + x_lo), y: 4, z: 4, core: 2. Of those that a mesh axis runs over, the one named last changes fastest.
Arguments:
- queries: bfloat16 [192, 4096], P('grp', 'side'), may hold values from -6 to 6
- kv_cache: bfloat16 [192, 16, 192, 256], P('grp', ('side', 'tp')), may hold values from -6 to 6
- lengths: int32 [192], P('grp'), may hold values from 2 to 768, as said below
- out_weight: bfloat16 [4096, 2048], P(('side', 'tp')), may hold values from -1 to 1
- resid: bfloat16 [192, 2048], P('grp'), may hold values from -6 to 6
- norm_gain: float32 [2048], replicated, may hold values from 0.1 to 1.9
- expert_ids: int32 [192, 8], P('grp'), may hold values from 0 to 127, all different within a row; in each aligned block of 24 rows (0 to 23, 24 to 47, ...) at most 3 rows name the same one
- expert_gates: float32 [192, 8], P('grp'), may hold values from 0.05 to 1
- w_gate_up: bfloat16 [128, 2048, 1536], P(('side', 'grp', 'tp')), may hold values from -0.125 to 0.125
- w_down: bfloat16 [128, 768, 2048], P(('side', 'grp', 'tp')), may hold values from -0.21875 to 0.21875
Outputs:
- layer_out: bfloat16 [192, 2048], P('grp', ('side', 'tp'))
Inputs may be any that keep to these rules, and one draw needn't show every extreme that they name: `lengths`: every row's cache holds at least two tokens; some row holds exactly 768. `expert_ids`: each row names 8 different experts. Among the rows of one row group no expert is named by more than 3 rows; in some group an expert is named by exactly 3.
All inputs are finite; a program needn't handle non-finite values.
Results may differ from a plain program's by a relative error of at most 0.017.
Values may be sent and summed in bfloat16 or wider, within the bound.
A program may use at most 64 MiB of HBM per device.

v0:
```python
import math
import jax
import jax.numpy as jnp
from jax import lax
from jax.sharding import PartitionSpec as P

QH = 32
KVH = 4
HD = 128
TOPK = 8


def swapped(value, axis, distance):
    mask = 2**distance
    pairs = [(source, source ^ mask) for source in range(lax.axis_size(axis))]
    return lax.ppermute(value, axis, pairs)


def body(
    queries,
    kv_cache,
    lengths,
    out_weight,
    resid,
    norm_gain,
    expert_ids,
    expert_gates,
    w_gate_up,
    w_down,
):
    lane_count = lax.axis_size("tp")
    tp_index = lax.axis_index("tp")
    side_count = lax.axis_size("side")
    section = lax.axis_index("side")
    grp_count = lax.axis_size("grp")
    group_size = side_count * lane_count
    member_index = section * lane_count + tp_index
    kv_parts = group_size // KVH
    group_heads = QH // KVH
    per_member = QH // group_size
    part_span = kv_cache.shape[2]
    model_width = out_weight.shape[1]
    piece_width = model_width // group_size
    rows_grp = lengths.shape[0]
    local_experts = w_gate_up.shape[0]
    experts_all = local_experts * side_count * grp_count * lane_count
    capacity = max(2, 2 * rows_grp * TOPK // experts_all)
    head_start = tp_index // kv_parts * group_heads * HD
    part_index = tp_index % kv_parts
    row_count = queries.shape[0]
    query_rows = lax.dynamic_slice_in_dim(queries, head_start, group_heads * HD, 1).reshape(
        row_count, group_heads, HD
    )
    key_rows = kv_cache[:, 0, :, :HD]
    value_rows = kv_cache[:, 0, :, HD:]
    positions = part_index * part_span + jnp.arange(part_span, dtype=jnp.int32)
    valid_mask = (positions[None, :] < lengths[:, None])[:, None, :]
    scores = jnp.einsum(
        "rgd,rpd->rgp", query_rows, key_rows, preferred_element_type=jnp.float32
    ) / math.sqrt(HD)
    scores = jnp.where(valid_mask, scores, -1e30)
    row_max = jnp.max(scores, axis=-1)
    for bit_index in range(kv_parts.bit_length() - 1):
        row_max = jnp.maximum(row_max, swapped(row_max, "tp", bit_index))
    weights = jnp.where(valid_mask, jnp.exp(scores - row_max[..., None]), 0.0)
    weight_sum = jnp.sum(weights, axis=-1)
    numerator = jnp.einsum(
        "rgp,rpd->rgd", weights.astype(jnp.bfloat16), value_rows, preferred_element_type=jnp.float32
    )
    for bit_index in range(kv_parts.bit_length() - 1):
        other_numerator, other_sum = swapped((numerator, weight_sum), "tp", bit_index)
        numerator = numerator + other_numerator
        weight_sum = weight_sum + other_sum
    heads_out = (numerator / weight_sum[..., None]).astype(jnp.bfloat16)
    mine = lax.dynamic_slice_in_dim(heads_out, part_index * per_member, per_member, 1).reshape(
        row_count, per_member * HD
    )
    projected = jnp.dot(mine, out_weight, preferred_element_type=jnp.float32)
    summed = lax.psum(projected, ("side", "tp"))
    middle = (resid.astype(jnp.float32) + summed).astype(jnp.bfloat16)
    middle_wide = middle.astype(jnp.float32)
    inv_rms = lax.rsqrt(jnp.mean(middle_wide * middle_wide, axis=-1, keepdims=True) + 1e-06)
    normed = (middle_wide * inv_rms * norm_gain).astype(jnp.bfloat16)
    column_experts = (
        (
            (section * grp_count + jnp.arange(grp_count, dtype=jnp.int32)[:, None]) * lane_count
            + tp_index
        )
        * local_experts
        + jnp.arange(local_experts, dtype=jnp.int32)[None, :]
    ).reshape(-1)
    matches = expert_ids[:, :, None] == column_experts[None, None, :]
    hit_count = jnp.sum(matches.astype(jnp.int32), axis=1)
    gate_cols = jnp.sum(jnp.where(matches, expert_gates[:, :, None], 0.0), axis=1)
    slot_rank = jnp.cumsum(hit_count, axis=0) - hit_count
    slot_ids = jnp.arange(capacity, dtype=jnp.int32)
    placed = (hit_count[:, :, None] == 1) & (slot_rank[:, :, None] == slot_ids[None, None, :])
    send_map = placed.astype(jnp.bfloat16)
    outgoing = jnp.einsum(
        "rcs,rd->csd", send_map, normed, preferred_element_type=jnp.float32
    ).astype(jnp.bfloat16)
    outgoing = outgoing.reshape(grp_count, local_experts, capacity, model_width)
    hidden = jnp.einsum(
        "gjcd,jdf->gjcf",
        lax.all_to_all(outgoing, "grp", split_axis=0, concat_axis=0, tiled=True),
        w_gate_up,
        preferred_element_type=jnp.float32,
    )
    inner_width = hidden.shape[-1] // 2
    activated = (jax.nn.silu(hidden[..., :inner_width]) * hidden[..., inner_width:]).astype(
        jnp.bfloat16
    )
    produced = jnp.einsum(
        "gjcf,jfd->gjcd", activated, w_down, preferred_element_type=jnp.float32
    ).astype(jnp.bfloat16)
    returned = lax.all_to_all(produced, "grp", split_axis=0, concat_axis=0, tiled=True)
    combine_weights = (send_map.astype(jnp.float32) * gate_cols[:, :, None]).reshape(row_count, -1)
    moe_part = jnp.dot(
        combine_weights,
        returned.reshape(-1, model_width).astype(jnp.float32),
        precision=lax.Precision.HIGHEST,
    )
    middle_mine = lax.dynamic_slice_in_dim(middle_wide, member_index * piece_width, piece_width, 1)
    moe_whole = lax.psum(moe_part, ("side", "tp"))
    return (
        middle_mine
        + lax.dynamic_slice_in_dim(moe_whole, member_index * piece_width, piece_width, 1)
    ).astype(jnp.bfloat16)


def solution(mesh):
    in_specs = (
        P("grp", "side"),
        P("grp", ("side", "tp"), None, None),
        P("grp"),
        P(("side", "tp"), None),
        P("grp", None),
        P(),
        P("grp", None),
        P("grp", None),
        P(("side", "grp", "tp"), None, None),
        P(("side", "grp", "tp"), None, None),
    )
    out_specs = P("grp", ("side", "tp"))
    return jax.shard_map(body, mesh=mesh, in_specs=in_specs, out_specs=out_specs, check_vma=False)
```

profile of v0, /device:TPU:1, one launch (start us, length us, event | category | flops | bytes accessed | tf_op | source)
XLA Modules:
  0.0 333.3 jit_solution(7118665528007655057)
XLA Ops:
  6.6 1.0 dynamic-slice_bitcast_fusion
  8.3 2.1 fusion.47
  10.3 2.5 collective-permute-start
  12.8 0.8 fusion.34
  13.9 3.4 %collective-permute-start.1 = (f32[24,8]{1,0:T(8,128)S(1)}, f32[24,8]{1,0:T(8,128)S(1)}, u32[]{:S(2)}, u32[]{:S(2)}) collective-permute-start(f32[24,8]{1,0:T(8,128)S(1)} %max.6), channel_id=1, source_target_pairs={{0,2},{1,3},{2,0},{3,1},{4,6},{5,7},{6,4},{7,5},{8,10},{9,11},{10,... | collective-permute-start | bytes 2312 | tf_op jit(solution)/shard_map/ppermute | solution.py:16
  18.7 1.0 collective-permute-start.4
  19.7 1.7 fusion.14
  22.0 2.9 collective-permute-start.5
  24.9 0.8 fusion.35
  25.9 1.1 collective-permute-done.5
  27.0 2.0 collective-permute-start.3
  29.1 2.9 collective-permute-done.3
  32.2 2.2 fusion.39
  34.4 1.3 convert_multiply_fusion
  35.7 130.8 %all-reduce.3.cloned.1.call-done = f32[24,2048]{1,0:T(8,128)} async-done(((f32[24,2048]{1,0:T(8,128)}), f32[24,2048]{1,0:T(8,128)}) %all-reduce.3.cloned.1.call-update) | async-done | bytes 196624 | tf_op jit(solution)/shard_map/psum | solution.py:79
  166.5 1.1 multiply_reduce_fusion
  167.5 0.9 fusion.10
  168.6 13.4 %all_to_all.10 = bf16[8,1,3,2048]{3,2,1,0:T(4,128)(2,1)S(1)} all-to-all(bf16[8,1,3,2048]{3,2,1,0:T(4,128)(2,1)S(1)} %copy.41), channel_id=1, replica_groups=mesh['side'=2,'grp'=8,'tp'=8] {'grp'}, dimensions={0} | all-to-all | bytes 196608 | tf_op jit(solution)/shard_map/all_to_all | solution.py:105
  182.0 3.7 %fusion.4 = f32[8,1,3,1536]{3,0,2,1:T(8,128)S(1)} fusion(bf16[1,2048,1536]{2,1,0:T(8,128)(2,1)} %param.18, bf16[8,1,3,2048]{3,2,1,0:T(4,128)(2,1)S(1)} %all_to_all.10), kind=kOutput, calls=%fused_computation.4 | convolution fusion | flops 150994944 | bytes 6537216 | tf_op jit(solution)/shard_map/gjcd,jdf->gjcf/dot_general | solution.py:103
  187.0 3.4 %all-to-all-start.1 = ((bf16[8,1,3,2048]{3,2,1,0:T(4,128)(2,1)}), bf16[8,1,3,2048]{3,2,1,0:T(4,128)(2,1)S(1)}, u32[]{:S(2)}, u32[]{:S(2)}) async-start(bf16[8,1,3,2048]{3,2,1,0:T(4,128)(2,1)} %copy.43), calls=%async_computation.1 | async-start | bytes 262144 | tf_op jit(solution)/shard_map/all_to_all | solution.py:116
  190.4 6.8 %all-to-all-done.1 = bf16[8,1,3,2048]{3,2,1,0:T(4,128)(2,1)S(1)} async-done(((bf16[8,1,3,2048]{3,2,1,0:T(4,128)(2,1)}), bf16[8,1,3,2048]{3,2,1,0:T(4,128)(2,1)S(1)}, u32[]{:S(2)}, u32[]{:S(2)}) %all-to-all-start.1) | async-done | bytes 98336 | tf_op jit(solution)/shard_map/all_to_all | solution.py:116
  197.9 1.9 fusion.48
  199.8 125.3 %all-reduce.5.cloned.1.call-done = f32[24,2048]{1,0:T(8,128)} async-done(((f32[24,2048]{1,0:T(8,128)}), f32[24,2048]{1,0:T(8,128)}) %all-reduce.5.cloned.1.call-update) | async-done | bytes 196624 | tf_op jit(solution)/shard_map/psum | solution.py:124
  325.1 1.3 add_convert_fusion.1
  (40 shorter events, 5.5 us)
Async XLA Ops:
  6.5 179.2 %copy-start = (bf16[1,768,2048]{2,1,0:T(8,128)(2,1)S(1)}, bf16[1,768,2048]{2,1,0:T(8,128)(2,1)}, u32[]{:S(2)}) copy-start(bf16[1,768,2048]{2,1,0:T(8,128)(2,1)} %param.19) | copy-start | bytes 9437188
  6.5 18.4 %copy-start.3 = (s32[24,8]{0,1:T(8,128)S(1)}, s32[24,8]{0,1:T(8,128)}, u32[]{:S(2)}) copy-start(s32[24,8]{0,1:T(8,128)} %param.16) | copy-start | bytes 2308
  6.5 159.9 %all-reduce.3.cloned.1.call-start = ((), (), s32[]{:S(2)}) async-start(), calls=%async_computation.2 | async-start | bytes 393216 | tf_op jit(solution)/shard_map/psum | solution.py:79
  8.3 158.2 %copy-start.1 = (bf16[24,2048]{1,0:T(8,128)(2,1)S(1)}, bf16[24,2048]{1,0:T(8,128)(2,1)}, u32[]{:S(2)}) copy-start(bf16[24,2048]{1,0:T(8,128)(2,1)} %param.14) | copy-start | bytes 294916
  10.3 3.6 %collective-permute-start = (f32[24,8]{1,0:T(8,128)S(1)}, f32[24,8]{1,0:T(8,128)S(1)}, u32[]{:S(2)}, u32[]{:S(2)}) collective-permute-start(f32[24,8]{1,0:T(8,128)S(1)} %get-tuple-element.9), channel_id=1, source_target_pairs={{0,1},{1,0},{2,3},{3,2},{4,5},{5,4},{6,7},{7,6},{8,9},{9,8},{10,11... | collective-permute-start | bytes 2312 | tf_op jit(solution)/shard_map/ppermute | solution.py:16
  13.9 4.6 %collective-permute-start.1 = (f32[24,8]{1,0:T(8,128)S(1)}, f32[24,8]{1,0:T(8,128)S(1)}, u32[]{:S(2)}, u32[]{:S(2)}) collective-permute-start(f32[24,8]{1,0:T(8,128)S(1)} %max.6), channel_id=1, source_target_pairs={{0,2},{1,3},{2,0},{3,1},{4,6},{5,7},{6,4},{7,5},{8,10},{9,11},{10,... | collective-permute-start | bytes 2312 | tf_op jit(solution)/shard_map/ppermute | solution.py:16
  18.7 3.3 collective-permute-start.4
  21.4 5.6 %collective-permute-start.2 = (f32[24,8,128]{2,1,0:T(8,128)S(1)}, f32[24,8,128]{2,1,0:T(8,128)S(1)}, u32[]{:S(2)}, u32[]{:S(2)}) collective-permute-start(f32[24,8,128]{2,1,0:T(8,128)S(1)} %fusion.14), channel_id=1, source_target_pairs={{0,1},{1,0},{2,3},{3,2},{4,5},{5,4},{6,7},{7,6},{8,9},{9,8},{10,11... | collective-permute-start | bytes 294920 | tf_op jit(solution)/shard_map/ppermute | solution.py:16
  22.0 5.0 %collective-permute-start.5 = (f32[24,8]{1,0:T(8,128)S(1)}, f32[24,8]{1,0:T(8,128)S(1)}, u32[]{:S(2)}, u32[]{:S(2)}) collective-permute-start(f32[24,8]{1,0:T(8,128)S(1)} %add.92), channel_id=1, source_target_pairs={{0,2},{1,3},{2,0},{3,1},{4,6},{5,7},{6,4},{7,5},{8,10},{9,11},{10,... | collective-permute-start | bytes 2312 | tf_op jit(solution)/shard_map/ppermute | solution.py:16
  27.0 5.1 %collective-permute-start.3 = (f32[24,8,128]{2,1,0:T(8,128)S(1)}, f32[24,8,128]{2,1,0:T(8,128)S(1)}, u32[]{:S(2)}, u32[]{:S(2)}) collective-permute-start(f32[24,8,128]{2,1,0:T(8,128)S(1)} %add.90), channel_id=1, source_target_pairs={{0,2},{1,3},{2,0},{3,1},{4,6},{5,7},{6,4},{7,5},{8,10},{9,11},{10,... | collective-permute-start | bytes 294920 | tf_op jit(solution)/shard_map/ppermute | solution.py:16
  185.7 4.7 %copy-start.2 = (f32[24,8,3]{0,2,1:T(4,128)S(1)}, f32[24,8,3]{0,2,1:T(4,128)}, u32[]{:S(2)}) copy-start(f32[24,8,3]{0,2,1:T(4,128)} %get-tuple-element.7) | copy-start | bytes 6916
  187.0 10.3 %all-to-all-start.1 = ((bf16[8,1,3,2048]{3,2,1,0:T(4,128)(2,1)}), bf16[8,1,3,2048]{3,2,1,0:T(4,128)(2,1)S(1)}, u32[]{:S(2)}, u32[]{:S(2)}) async-start(bf16[8,1,3,2048]{3,2,1,0:T(4,128)(2,1)} %copy.43), calls=%async_computation.1 | async-start | bytes 262144 | tf_op jit(solution)/shard_map/all_to_all | solution.py:116
  190.3 134.8 %all-reduce.5.cloned.1.call-start = ((), (), s32[]{:S(2)}) async-start(), calls=%async_computation.3 | async-start | bytes 393216 | tf_op jit(solution)/shard_map/psum | solution.py:124
Sparse Core Ops, SparseCore 0:
  34.5 131.9 all-reduce.2
  199.9 125.1 all-reduce.4
where the time goes:
time: 334 us; the launch traced here: 333 us
  waiting for transfers between devices  268 us (80%)
  starting transfers between devices  15.9 us (5%)
  between operations  13.5 us (4%)
  blocking collectives  13.4 us (4%)
  matrix products  13 us (4%)
  other arithmetic  6.89 us (2%)
    psum x1, waiting for transfers between devices, body(): summed = lax.psum(projected, ('side', 'tp'))  131 us
    psum x1, waiting for transfers between devices, body(): moe_whole = lax.psum(moe_part, ('side', 'tp'))  125 us
    all_to_all x1, blocking collectives, body(): lax.all_to_all(outgoing, 'grp', split_axis=0, concat_axis=0, tiled=True)  13.4 us
    ppermute x6, starting transfers between devices, swapped(): return lax.ppermute(value, axis, pairs)  12.4 us
    all_to_all x1, waiting for transfers between devices, body(): lax.all_to_all(produced, 'grp', split_axis=0, concat_axis=0, tiled=True)  6.8 us
  transfers between devices with their start and end apart: 9, of which 7 were waited for; matrix products, arithmetic and copies ran while one was open for 2% of the time, Pallas kernels for 0%

commit v1 on v0

--- a/solution.py
+++ b/solution.py
@@ -76,7 +76,8 @@
         row_count, per_member * HD
     )
     projected = jnp.dot(mine, out_weight, preferred_element_type=jnp.float32)
-    summed = lax.psum(projected, ("side", "tp"))
+    inner = lax.psum(projected, "tp")
+    summed = lax.psum(inner, "side")
     middle = (resid.astype(jnp.float32) + summed).astype(jnp.bfloat16)
     middle_wide = middle.astype(jnp.float32)
     inv_rms = lax.rsqrt(jnp.mean(middle_wide * middle_wide, axis=-1, keepdims=True) + 1e-06)

time: 334 us -> 308 us (0.922)
  waiting for transfers between devices: 268 us -> 244 us
    psum x1 -> x2, waiting for transfers between devices: 131 us -> 105 us  [the longest x1 74.9 us: body(): inner = lax.psum(projected, 'tp')]
  transfers between devices with their start and end apart: 9 -> 10, of which waited for: 7 -> 8; matrix products, arithmetic and copies ran while one was open for 2% -> 1% of each run, Pallas kernels for 0% -> 0%
where the time goes in v1:
time: 308 us; the launch traced here: 307 us
  waiting for transfers between devices  244 us (79%)
  starting transfers between devices  15.9 us (5%)
  blocking collectives  13.3 us (4%)
  between operations  13.2 us (4%)
  matrix products  13 us (4%)
  other arithmetic  4.98 us (2%)
    psum x1, waiting for transfers between devices, body(): moe_whole = lax.psum(moe_part, ('side', 'tp'))  126 us
    psum x1, waiting for transfers between devices, body(): inner = lax.psum(projected, 'tp')  74.9 us
    psum x1, waiting for transfers between devices, body(): summed = lax.psum(inner, 'side')  30.4 us
    all_to_all x1, blocking collectives, body(): lax.all_to_all(outgoing, 'grp', split_axis=0, concat_axis=0, tiled=True)  13.3 us
    ppermute x6, starting transfers between devices, swapped(): return lax.ppermute(value, axis, pairs)  12.4 us
    all_to_all x1, waiting for transfers between devices, body(): lax.all_to_all(produced, 'grp', split_axis=0, concat_axis=0, tiled=True)  6.8 us
    ppermute x6, waiting for transfers between devices, swapped(): return lax.ppermute(value, axis, pairs)  6.2 us
  transfers between devices with their start and end apart: 10, of which 8 were waited for; matrix products, arithmetic and copies ran while one was open for 1% of the time, Pallas kernels for 0%

profile of v1, /device:TPU:1, one launch (start us, length us, event | category | flops | bytes accessed | tf_op | source)
XLA Modules:
  0.0 307.0 jit_solution(18003189197908842500)
XLA Ops:
  6.6 1.0 dynamic-slice_bitcast_fusion
  8.3 2.1 fusion.47
  10.3 2.5 collective-permute-start
  12.8 1.1 collective-permute-done
  13.9 3.4 %collective-permute-start.1 = (f32[24,8]{1,0:T(8,128)S(1)}, f32[24,8]{1,0:T(8,128)S(1)}, u32[]{:S(2)}, u32[]{:S(2)}) collective-permute-start(f32[24,8]{1,0:T(8,128)S(1)} %max.6), channel_id=1, source_target_pairs={{0,2},{1,3},{2,0},{3,1},{4,6},{5,7},{6,4},{7,5},{8,10},{9,11},{10,... | collective-permute-start | bytes 2312 | tf_op jit(solution)/shard_map/ppermute | solution.py:16
  17.3 0.8 fusion.35
  18.7 1.0 collective-permute-start.4
  19.7 1.7 fusion.14
  22.0 2.9 collective-permute-start.5
  25.2 1.8 collective-permute-done.5
  27.0 2.0 collective-permute-start.3
  29.1 2.9 collective-permute-done.3
  32.2 2.2 fusion.39
  34.4 74.9 %all-reduce.4.cloned.1.call-done = f32[24,2048]{1,0:T(8,128)} async-done(((f32[24,2048]{1,0:T(8,128)}), f32[24,2048]{1,0:T(8,128)}) %all-reduce.4.cloned.1.call-update) | async-done | bytes 196624 | tf_op jit(solution)/shard_map/psum | solution.py:79
  110.0 30.4 %all-reduce.6.cloned.1.call-done = f32[24,2048]{1,0:T(8,128)} async-done(((f32[24,2048]{1,0:T(8,128)}), f32[24,2048]{1,0:T(8,128)}) %all-reduce.6.cloned.1.call-update) | async-done | bytes 196624 | tf_op jit(solution)/shard_map/psum | solution.py:80
  140.4 1.1 multiply_reduce_fusion
  141.5 0.9 fusion.10
  142.5 13.3 %all_to_all.10 = bf16[8,1,3,2048]{3,2,1,0:T(4,128)(2,1)S(1)} all-to-all(bf16[8,1,3,2048]{3,2,1,0:T(4,128)(2,1)S(1)} %copy.41), channel_id=1, replica_groups=mesh['side'=2,'grp'=8,'tp'=8] {'grp'}, dimensions={0} | all-to-all | bytes 196608 | tf_op jit(solution)/shard_map/all_to_all | solution.py:106
  155.8 3.7 %fusion.4 = f32[8,1,3,1536]{3,0,2,1:T(8,128)S(1)} fusion(bf16[1,2048,1536]{2,1,0:T(8,128)(2,1)} %param.18, bf16[8,1,3,2048]{3,2,1,0:T(4,128)(2,1)S(1)} %all_to_all.10), kind=kOutput, calls=%fused_computation.4 | convolution fusion | flops 150994944 | bytes 6537216 | tf_op jit(solution)/shard_map/gjcd,jdf->gjcf/dot_general | solution.py:104
  160.8 3.4 %all-to-all-start.1 = ((bf16[8,1,3,2048]{3,2,1,0:T(4,128)(2,1)}), bf16[8,1,3,2048]{3,2,1,0:T(4,128)(2,1)S(1)}, u32[]{:S(2)}, u32[]{:S(2)}) async-start(bf16[8,1,3,2048]{3,2,1,0:T(4,128)(2,1)} %copy.43), calls=%async_computation.1 | async-start | bytes 262144 | tf_op jit(solution)/shard_map/all_to_all | solution.py:117
  164.3 6.8 %all-to-all-done.1 = bf16[8,1,3,2048]{3,2,1,0:T(4,128)(2,1)S(1)} async-done(((bf16[8,1,3,2048]{3,2,1,0:T(4,128)(2,1)}), bf16[8,1,3,2048]{3,2,1,0:T(4,128)(2,1)S(1)}, u32[]{:S(2)}, u32[]{:S(2)}) %all-to-all-start.1) | async-done | bytes 98336 | tf_op jit(solution)/shard_map/all_to_all | solution.py:117
  171.8 1.9 fusion.48
  173.7 125.5 %all-reduce.8.cloned.1.call-done = f32[24,2048]{1,0:T(8,128)} async-done(((f32[24,2048]{1,0:T(8,128)}), f32[24,2048]{1,0:T(8,128)}) %all-reduce.8.cloned.1.call-update) | async-done | bytes 196624 | tf_op jit(solution)/shard_map/psum | solution.py:125
  299.2 1.3 add_convert_fusion.1
  (43 shorter events, 5.2 us)
Async XLA Ops:
  6.5 153.0 %copy-start = (bf16[1,768,2048]{2,1,0:T(8,128)(2,1)S(1)}, bf16[1,768,2048]{2,1,0:T(8,128)(2,1)}, u32[]{:S(2)}) copy-start(bf16[1,768,2048]{2,1,0:T(8,128)(2,1)} %param.19) | copy-start | bytes 9437188
  6.5 18.4 %copy-start.3 = (s32[24,8]{0,1:T(8,128)S(1)}, s32[24,8]{0,1:T(8,128)}, u32[]{:S(2)}) copy-start(s32[24,8]{0,1:T(8,128)} %param.16) | copy-start | bytes 2308
  6.5 102.8 %all-reduce.4.cloned.1.call-start = ((), (), s32[]{:S(2)}) async-start(), calls=%async_computation.2 | async-start | bytes 393216 | tf_op jit(solution)/shard_map/psum | solution.py:79
  10.3 130.1 %copy-start.1 = (bf16[24,2048]{1,0:T(8,128)(2,1)S(1)}, bf16[24,2048]{1,0:T(8,128)(2,1)}, u32[]{:S(2)}) copy-start(bf16[24,2048]{1,0:T(8,128)(2,1)} %param.14) | copy-start | bytes 294916
  10.3 3.6 %collective-permute-start = (f32[24,8]{1,0:T(8,128)S(1)}, f32[24,8]{1,0:T(8,128)S(1)}, u32[]{:S(2)}, u32[]{:S(2)}) collective-permute-start(f32[24,8]{1,0:T(8,128)S(1)} %get-tuple-element.9), channel_id=1, source_target_pairs={{0,1},{1,0},{2,3},{3,2},{4,5},{5,4},{6,7},{7,6},{8,9},{9,8},{10,11... | collective-permute-start | bytes 2312 | tf_op jit(solution)/shard_map/ppermute | solution.py:16
  13.9 4.6 %collective-permute-start.1 = (f32[24,8]{1,0:T(8,128)S(1)}, f32[24,8]{1,0:T(8,128)S(1)}, u32[]{:S(2)}, u32[]{:S(2)}) collective-permute-start(f32[24,8]{1,0:T(8,128)S(1)} %max.6), channel_id=1, source_target_pairs={{0,2},{1,3},{2,0},{3,1},{4,6},{5,7},{6,4},{7,5},{8,10},{9,11},{10,... | collective-permute-start | bytes 2312 | tf_op jit(solution)/shard_map/ppermute | solution.py:16
  18.7 3.3 %collective-permute-start.4 = (f32[24,8]{1,0:T(8,128)S(1)}, f32[24,8]{1,0:T(8,128)S(1)}, u32[]{:S(2)}, u32[]{:S(2)}) collective-permute-start(f32[24,8]{1,0:T(8,128)S(1)} %fusion.18), channel_id=1, source_target_pairs={{0,1},{1,0},{2,3},{3,2},{4,5},{5,4},{6,7},{7,6},{8,9},{9,8},{10,11... | collective-permute-start | bytes 2312 | tf_op jit(solution)/shard_map/ppermute | solution.py:16
  21.4 5.6 %collective-permute-start.2 = (f32[24,8,128]{2,1,0:T(8,128)S(1)}, f32[24,8,128]{2,1,0:T(8,128)S(1)}, u32[]{:S(2)}, u32[]{:S(2)}) collective-permute-start(f32[24,8,128]{2,1,0:T(8,128)S(1)} %fusion.14), channel_id=1, source_target_pairs={{0,1},{1,0},{2,3},{3,2},{4,5},{5,4},{6,7},{7,6},{8,9},{9,8},{10,11... | collective-permute-start | bytes 294920 | tf_op jit(solution)/shard_map/ppermute | solution.py:16
  22.0 5.0 %collective-permute-start.5 = (f32[24,8]{1,0:T(8,128)S(1)}, f32[24,8]{1,0:T(8,128)S(1)}, u32[]{:S(2)}, u32[]{:S(2)}) collective-permute-start(f32[24,8]{1,0:T(8,128)S(1)} %add.94), channel_id=1, source_target_pairs={{0,2},{1,3},{2,0},{3,1},{4,6},{5,7},{6,4},{7,5},{8,10},{9,11},{10,... | collective-permute-start | bytes 2312 | tf_op jit(solution)/shard_map/ppermute | solution.py:16
  27.0 5.1 %collective-permute-start.3 = (f32[24,8,128]{2,1,0:T(8,128)S(1)}, f32[24,8,128]{2,1,0:T(8,128)S(1)}, u32[]{:S(2)}, u32[]{:S(2)}) collective-permute-start(f32[24,8,128]{2,1,0:T(8,128)S(1)} %add.92), channel_id=1, source_target_pairs={{0,2},{1,3},{2,0},{3,1},{4,6},{5,7},{6,4},{7,5},{8,10},{9,11},{10,... | collective-permute-start | bytes 294920 | tf_op jit(solution)/shard_map/ppermute | solution.py:16
  34.4 106.1 %all-reduce.6.cloned.1.call-start = ((), (), s32[]{:S(2)}) async-start(), calls=%async_computation.3 | async-start | bytes 393216 | tf_op jit(solution)/shard_map/psum | solution.py:80
  159.5 4.7 %copy-start.2 = (f32[24,8,3]{0,2,1:T(4,128)S(1)}, f32[24,8,3]{0,2,1:T(4,128)}, u32[]{:S(2)}) copy-start(f32[24,8,3]{0,2,1:T(4,128)} %get-tuple-element.7) | copy-start | bytes 6916
  160.8 10.2 %all-to-all-start.1 = ((bf16[8,1,3,2048]{3,2,1,0:T(4,128)(2,1)}), bf16[8,1,3,2048]{3,2,1,0:T(4,128)(2,1)S(1)}, u32[]{:S(2)}, u32[]{:S(2)}) async-start(bf16[8,1,3,2048]{3,2,1,0:T(4,128)(2,1)} %copy.43), calls=%async_computation.1 | async-start | bytes 262144 | tf_op jit(solution)/shard_map/all_to_all | solution.py:117
  164.2 135.0 %all-reduce.8.cloned.1.call-start = ((), (), s32[]{:S(2)}) async-start(), calls=%async_computation.4 | async-start | bytes 393216 | tf_op jit(solution)/shard_map/psum | solution.py:125
Sparse Core Ops, SparseCore 0:
  34.5 74.8 all-reduce.3
  111.9 28.4 all-reduce.5
  173.8 125.3 all-reduce.7
